TPU v7x, 256 devices: a whole 4x4x8 slice. The times are simulated.
256 devices in a mesh: genome: 32 (over z, x), anc: 4 (over y_lo, core), trait: 2 (over y_hi).
Axes of the slice: x: 4, y: 4 (y_hi: 2, y_lo: 2; y = y_hi * 2 + y_lo), z: 8, core: 2. Of those that a mesh axis runs over, the one named last changes fastest.
Arguments:
- coefficients: float32 [4, 128, 65536], P('anc', 'trait', 'genome'), may hold values from -3 to 3
- sumstats: float32 [4, 128, 65536], P('anc', 'trait', 'genome'), may hold values from -12 to 12
- linkage: bfloat16 [4, 65536, 4096], P('anc', 'genome'), may hold values from -0.09375 to 0.09375
- band_start: int32 [4, 256], P('anc', 'genome'), may hold values from 0 to 61440, as said below
- group_ids: int32 [4, 65536], P('anc', 'genome'), may hold values from 0 to 63, never falling along the last dimension, each value on 1 to 8192 neighbouring positions
- group_weight: float32 [4, 64], P('anc'), may hold values from 0.1 to 1.5
- dosage: bfloat16 [4, 2048, 65536], P('anc', None, 'genome'), may hold values from 0 to 2
Outputs:
- updated: float32 [4, 128, 65536], P('anc', 'trait', 'genome')
- scores: float32 [4, 128, 2048], P('anc', 'trait', 'genome')
Inputs may be any that keep to these rules, and one draw needn't show every extreme that they name: band_start[a, u] is the first of the 4096 consecutive SNP columns stored in linkage[a] for row block u, the SNPs u * 256 to u * 256 + 255; these columns always include the block's own SNPs. `group_ids`: group ids never fall along the SNPs of an ancestry, so each group is one run of consecutive SNPs.
All inputs are finite; a program needn't handle non-finite values.
Results may differ from a plain program's by a relative error of at most 0.003.
Values may be sent and summed in bfloat16 or wider, within the bound.
No kernel may reach another device: no remote copies, remote signals or barrier semaphores. Data moves between devices by JAX's collectives and lax.ppermute only.
A program may use at most 128 MiB of HBM per device.

v0:
```python
import math
import jax
import jax.numpy as jnp
from jax import lax
from jax.sharding import PartitionSpec as P

TRAITS = 128
TILE = 256
step_size = 0.5
merging = 0.5
epsilon = 1e-06


def total_of_pieces(value, axis):
    parts = lax.all_gather(value, axis)
    return parts.sum(axis=0)


def passed_along(block, axis, distance):
    devices = range(lax.axis_size(axis))
    route = [(i - distance, i) for i in devices if i - distance in devices]
    return lax.ppermute(block, axis, route)


def sent_to_all(value, axis):
    copies = jnp.broadcast_to(value, (lax.axis_size(axis), *value.shape))
    return lax.all_to_all(copies, axis, split_axis=0, concat_axis=0, tiled=True)


def over_copies(value, axis):
    return sent_to_all(value, axis).sum(axis=0)


def rows_first(arrays, axis, dims):
    turned = [jnp.moveaxis(a, dim, 0) for a, dim in zip(arrays, dims)]
    both = jnp.concatenate([t.reshape(len(t), -1) for t in turned], axis=1)
    result, at, done = (lax.all_gather(both, axis, axis=0, tiled=True), 0, [])
    for t, dim in zip(turned, dims):
        piece = result[:, at : at + t[0].size].reshape(-1, *t.shape[1:])
        done.append(jnp.moveaxis(piece, 0, dim))
        at += t[0].size
    return tuple(done)


def cut_along(value, dim, peers):
    dims = value.shape
    parts = value.reshape(*dims[:dim], peers, dims[dim] // peers, *dims[dim + 1 :])
    return jnp.moveaxis(parts, dim, 0)


def sent_and_summed(value, axis, dim):
    parts = cut_along(value, dim, lax.axis_size(axis))
    arrived = lax.all_to_all(parts, axis, split_axis=0, concat_axis=0, tiled=True)
    return arrived.sum(axis=0)


def per_device(coefficients, sumstats, linkage, band_start, group_ids, group_weight, dosage):
    current = coefficients[0]
    targets = sumstats[0]
    band = linkage[0]
    starts = band_start[0]
    group_list = group_ids[0]
    weights = group_weight[0]
    genotype = dosage[0]
    traits_here, snp_rows = current.shape
    band_width = band.shape[1]
    reach_count = band_width // snp_rows
    genome_count = lax.axis_size("genome")
    position = lax.axis_index("genome")
    anchor = position * snp_rows
    ancestries = lax.axis_size("anc") * coefficients.shape[0]
    mean_coef = total_of_pieces(current, "anc") / ancestries
    low_copy = current.astype(jnp.bfloat16)
    below_list = []
    above_list = []
    for distance in range(1, reach_count + 1):
        below_list.insert(0, passed_along(low_copy, "genome", distance))
        above_list.append(passed_along(low_copy, "genome", -distance))
    extended = jnp.concatenate(below_list + [low_copy] + above_list, axis=1)
    local_start = starts - anchor + band_width
    windows = jax.vmap(
        lambda begin_at: lax.dynamic_slice_in_dim(extended, begin_at, band_width, 1)
    )(local_start)
    band_tiles = band.reshape(snp_rows // TILE, TILE, band_width)
    products = jnp.einsum("ntw,nrw->tnr", windows, band_tiles, preferred_element_type=jnp.float32)
    band_product = products.reshape(traits_here, snp_rows)
    gradient = current + band_product - targets + merging * (current - mean_coef)
    proposal = current - step_size * gradient
    trait_part = jnp.sum(proposal * proposal, axis=0)
    trait_total = over_copies(trait_part, "trait")
    same_group = (group_list[:, None] == group_list[None, :]).astype(jnp.float32)
    local_squares = jnp.dot(same_group, trait_total, precision=lax.Precision.HIGHEST)
    local_counts = jnp.sum(same_group, axis=1)
    id_float = group_list.astype(jnp.float32)
    first_id = id_float[0]
    last_id = id_float[-1]
    edge_values = rows_first(
        (
            first_id[None],
            last_id[None],
            local_squares[:1],
            local_counts[:1],
            local_squares[-1:],
            local_counts[-1:],
        ),
        "genome",
        (0, 0, 0, 0, 0, 0),
    )
    firsts, lasts, head_squares, head_counts, tail_squares, tail_counts = edge_values
    others = (jnp.arange(genome_count, dtype=jnp.int32) != position)[None, :]
    at_head = id_float[:, None] == firsts[None, :]
    at_tail = id_float[:, None] == lasts[None, :]
    square_terms = jnp.where(
        at_head, head_squares[None, :], jnp.where(at_tail, tail_squares[None, :], 0.0)
    )
    count_terms = jnp.where(
        at_head, head_counts[None, :], jnp.where(at_tail, tail_counts[None, :], 0.0)
    )
    extra_squares = jnp.sum(jnp.where(others, square_terms, 0.0), axis=1)
    extra_counts = jnp.sum(jnp.where(others, count_terms, 0.0), axis=1)
    group_squares = local_squares + extra_squares
    group_counts = local_counts + extra_counts
    lookup = (group_list[:, None] == jnp.arange(weights.shape[0], dtype=jnp.int32)[None, :]).astype(
        jnp.float32
    )
    snp_weight = jnp.dot(lookup, weights, precision=lax.Precision.HIGHEST)
    threshold = step_size * snp_weight * jnp.sqrt(group_counts * TRAITS)
    factor = jnp.maximum(0.0, 1.0 - threshold / jnp.sqrt(group_squares + epsilon))
    updated = proposal * factor[None, :]
    snps_total = snp_rows * genome_count
    partial_value = lax.dot_general(
        updated.astype(jnp.bfloat16),
        genotype,
        (((1,), (1,)), ((), ())),
        preferred_element_type=jnp.float32,
    ) / math.sqrt(snps_total)
    scores = sent_and_summed(partial_value, "genome", 1)
    return (updated[None], scores[None])


def solution(mesh):
    in_specs = (
        P("anc", "trait", "genome"),
        P("anc", "trait", "genome"),
        P("anc", "genome", None),
        P("anc", "genome"),
        P("anc", "genome"),
        P("anc", None),
        P("anc", None, "genome"),
    )
    out_specs = (P("anc", "trait", "genome"), P("anc", "trait", "genome"))
    return jax.shard_map(
        per_device, mesh=mesh, in_specs=in_specs, out_specs=out_specs, check_vma=False
    )
```

profile of v0, /device:TPU:32, one launch (start us, length us, event | category | flops | bytes accessed | tf_op | source)
XLA Modules:
  0.0 168.4 jit_solution(14491899200398587660)
XLA Ops:
  8.3 4.9 %collective-permute-start = (bf16[64,2048]{1,0:T(8,128)(2,1)S(1)}, bf16[64,2048]{1,0:T(8,128)(2,1)S(1)}, u32[]{:S(2)}, u32[]{:S(2)}) collective-permute-start(bf16[64,2048]{1,0:T(8,128)(2,1)S(1)} %bitcast_convert_fusion), channel_id=1, source_target_pairs={{0,16},{8,24},{16,32},{24,40},{32,48},{40,56},{48,64},{56,72},{64,... | collective-permute-start | bytes 786440 | tf_op jit(solution)/shard_map/ppermute | solution.py:22
  13.2 2.5 %collective-permute-start.1 = (bf16[64,2048]{1,0:T(8,128)(2,1)S(1)}, bf16[64,2048]{1,0:T(8,128)(2,1)S(1)}, u32[]{:S(2)}, u32[]{:S(2)}) collective-permute-start(bf16[64,2048]{1,0:T(8,128)(2,1)S(1)} %bitcast_convert_fusion), channel_id=1, source_target_pairs={{0,8},{8,16},{16,24},{24,32},{32,40},{40,48},{48,56},{56,64},{64,7... | collective-permute-start | bytes 786440 | tf_op jit(solution)/shard_map/ppermute | solution.py:22
  15.7 5.5 %collective-permute-start.2 = (bf16[64,2048]{1,0:T(8,128)(2,1)S(1)}, bf16[64,2048]{1,0:T(8,128)(2,1)S(1)}, u32[]{:S(2)}, u32[]{:S(2)}) collective-permute-start(bf16[64,2048]{1,0:T(8,128)(2,1)S(1)} %bitcast_convert_fusion), channel_id=1, source_target_pairs={{8,0},{16,8},{24,16},{32,24},{40,32},{48,40},{56,48},{64,56},{72,6... | collective-permute-start | bytes 786440 | tf_op jit(solution)/shard_map/ppermute | solution.py:22
  21.2 1.9 %collective-permute-start.3 = (bf16[64,2048]{1,0:T(8,128)(2,1)S(1)}, bf16[64,2048]{1,0:T(8,128)(2,1)S(1)}, u32[]{:S(2)}, u32[]{:S(2)}) collective-permute-start(bf16[64,2048]{1,0:T(8,128)(2,1)S(1)} %bitcast_convert_fusion), channel_id=1, source_target_pairs={{16,0},{24,8},{32,16},{40,24},{48,32},{56,40},{64,48},{72,56},{80,... | collective-permute-start | bytes 786440 | tf_op jit(solution)/shard_map/ppermute | solution.py:22
  23.2 2.5 %fusion.2 = f32[2048]{0:T(1024)S(1)} fusion(s32[2048]{0:T(1024)} %bitcast.93), kind=kLoop, calls=%fused_computation.5 | loop fusion | flops 12580864 | bytes 16384 | tf_op jit(solution)/shard_map/reduce_sum | solution.py:93
  30.9 1.9 %collective-permute-done.3 = bf16[64,2048]{1,0:T(8,128)(2,1)S(1)} collective-permute-done((bf16[64,2048]{1,0:T(8,128)(2,1)S(1)}, bf16[64,2048]{1,0:T(8,128)(2,1)S(1)}, u32[]{:S(2)}, u32[]{:S(2)}) %collective-permute-start.3) | collective-permute-done | bytes 262176 | tf_op jit(solution)/shard_map/ppermute | solution.py:22
  32.8 18.1 %while.1 = (s32[]{:T(128)}, bf16[64,10240]{1,0:T(8,128)(2,1)S(1)}, s32[8,2]{0,1:T(2,128)S(1)}, bf16[8,64,4096]{2,1,0:T(8,128)(2,1)}, s32[]{:T(128)}) while((s32[]{:T(128)}, bf16[64,10240]{1,0:T(8,128)(2,1)S(1)}, s32[8,2]{0,1:T(2,128)S(1)}, bf16[8,64,4096]{2,1,0:T(8,128)(2,1)}, s32[]{:T(128)}) %tuple.29), condition=%wide.while_cond, body=%wide.while_body.sunk | while | flops 2 | bytes 1049689 | solution.py:82
  35.7 1.7 bitcast_dynamic-update-slice_fusion.2
  37.9 1.7 bitcast_dynamic-update-slice_fusion.2
  40.2 1.7 bitcast_dynamic-update-slice_fusion.2
  42.5 1.6 bitcast_dynamic-update-slice_fusion.2
  44.7 1.7 bitcast_dynamic-update-slice_fusion.2
  47.0 1.6 bitcast_dynamic-update-slice_fusion.2
  49.3 1.7 bitcast_dynamic-update-slice_fusion.2
  50.9 12.4 %fusion.33 = f32[8,64,256]{2,1,0:T(8,128)S(1)} fusion(bf16[8,64,4096]{2,1,0:T(8,128)(2,1)} %get-tuple-element.9, bf16[8,256,4096]{2,1,0:T(8,128)(2,1)} %bitcast.83), kind=kOutput, calls=%fused_computation.59 | convolution fusion | flops 1073741824 | bytes 21495808 | tf_op jit(solution)/shard_map/ntw,nrw->tnr/dot_general | solution.py:85
  63.4 1.8 %reduce_sum.63 = f32[64,2048]{1,0:T(8,128)S(1)} reduce(f32[4,64,2048]{2,1,0:T(8,128)} %all-gather.3.cloned.1.call-done, f32[]{:T(128)} %constant.8.clone.1), dimensions={0}, to_apply=%region_0.0 | reduce | flops 393216 | bytes 2621444 | tf_op jit(solution)/shard_map/reduce_sum | solution.py:16
  66.0 4.5 %all-to-all-start = ((f32[2,1,2048]{2,1,0:T(1,128)}), f32[2,1,2048]{2,1,0:T(1,128)S(1)}, u32[]{:S(2)}, u32[]{:S(2)}) async-start(f32[2,1,2048]{2,1,0:T(1,128)} %broadcast_in_dim.67), calls=%async_computation | async-start | bytes 32768 | tf_op jit(solution)/shard_map/all_to_all | solution.py:27
  70.9 5.0 %all-to-all-done = f32[2,1,2048]{2,1,0:T(1,128)S(1)} async-done(((f32[2,1,2048]{2,1,0:T(1,128)}), f32[2,1,2048]{2,1,0:T(1,128)S(1)}, u32[]{:S(2)}, u32[]{:S(2)}) %all-to-all-start) | async-done | bytes 16416 | tf_op jit(solution)/shard_map/all_to_all | solution.py:27
  75.9 6.9 %fusion = f32[1,2048]{1,0:T(1,128)S(1)} fusion(f32[2048,1]{0,1:T(1,128)S(1)} %bitcast.92, s32[2048]{0:T(1024)S(1)} %bitcast.96), kind=kOutput, calls=%fused_computation.2 | convolution fusion | flops 54525952 | bytes 24576 | tf_op jit(solution)/shard_map/dot_general | solution.py:92
  83.4 3.9 %concatenate.11 = f32[1,6]{1,0:T(1,128)S(1)} concatenate(f32[1,1]{1,0:T(1,128)} %bitcast.10, f32[1,1]{1,0:T(1,128)} %bitcast.11, f32[1,1]{1,0:T(1,128)} %bitcast.15, f32[1,1]{1,0:T(1,128)} %bitcast.16, f32[1,1]{1,0:T(1,128)} %bitcast.17, f32[1,1]{1,0:T(1,128)} %bitcast.18), dimensions={1} | concatenate | bytes 48 | tf_op jit(solution)/shard_map/concatenate | solution.py:36
  87.4 42.7 %all-gather = f32[32,1,6]{2,1,0:T(1,128)S(1)} all-gather(f32[1,1,6]{2,1,0:T(1,128)S(1)} %bitcast.98), channel_id=1, replica_groups=mesh['genome'=32,'anc'=4,'trait'=2] {'genome'}, dimensions={0}, use_global_device_ids=true | all-gather | bytes 792 | tf_op jit(solution)/shard_map/all_gather | solution.py:37
  130.8 6.2 %fusion.7 = f32[64,2048]{1,0:T(8,128)S(1)} fusion(bf16[1,2048,2048]{2,1,0:T(8,128)(2,1)} %param.13, f32[1,64,2048]{2,1,0:T(8,128)S(1)} %fusion.20), kind=kOutput, calls=%fused_computation.10 | convolution fusion | flops 537133056 | bytes 9437184 | tf_op jit(solution)/shard_map/dot_general | solution.py:131
  138.7 19.3 %all_to_all.11 = f32[32,1,4096]{2,1,0:T(1,128)S(1)} all-to-all(f32[32,1,4096]{2,1,0:T(1,128)S(1)} %reshape.135), channel_id=1, replica_groups=mesh['genome'=32,'anc'=4,'trait'=2] {'genome'}, dimensions={0} | all-to-all | bytes 1048576 | tf_op jit(solution)/shard_map/all_to_all | solution.py:53
  158.5 1.9 %reduce.13 = f32[32,4096]{1,0:T(8,128)S(1)} reduce(f32[32,1,4096]{2,1,0:T(1,128)S(1)} %all_to_all.11, f32[]{:T(128)} %broadcast.110), dimensions={1}, to_apply=%all_to_all.8.reduce_sub_computation | reduce | bytes 1048580 | tf_op jit(solution)/shard_map/all_to_all | solution.py:53
  (64 shorter events, 18.7 us)
Async XLA Ops:
  7.2 18.5 %copy-start = (f32[1,64]{1,0:T(1,128)S(1)}, f32[1,64]{1,0:T(1,128)}, u32[]{:S(2)}) copy-start(f32[1,64]{1,0:T(1,128)} %param.12) | copy-start | bytes 772
  7.2 56.2 %all-gather.3.cloned.1.call-start = ((), (), s32[]{:S(2)}) async-start(), calls=%async_computation.2 | async-start | bytes 2621440 | tf_op jit(solution)/shard_map/all_gather | solution.py:15
  8.3 21.4 %collective-permute-start = (bf16[64,2048]{1,0:T(8,128)(2,1)S(1)}, bf16[64,2048]{1,0:T(8,128)(2,1)S(1)}, u32[]{:S(2)}, u32[]{:S(2)}) collective-permute-start(bf16[64,2048]{1,0:T(8,128)(2,1)S(1)} %bitcast_convert_fusion), channel_id=1, source_target_pairs={{0,16},{8,24},{16,32},{24,40},{32,48},{40,56},{48,64},{56,72},{64,... | collective-permute-start | bytes 786440 | tf_op jit(solution)/shard_map/ppermute | solution.py:22
  13.2 16.5 %collective-permute-start.1 = (bf16[64,2048]{1,0:T(8,128)(2,1)S(1)}, bf16[64,2048]{1,0:T(8,128)(2,1)S(1)}, u32[]{:S(2)}, u32[]{:S(2)}) collective-permute-start(bf16[64,2048]{1,0:T(8,128)(2,1)S(1)} %bitcast_convert_fusion), channel_id=1, source_target_pairs={{0,8},{8,16},{16,24},{24,32},{32,40},{40,48},{48,56},{56,64},{64,7... | collective-permute-start | bytes 786440 | tf_op jit(solution)/shard_map/ppermute | solution.py:22
  15.7 15.1 %collective-permute-start.2 = (bf16[64,2048]{1,0:T(8,128)(2,1)S(1)}, bf16[64,2048]{1,0:T(8,128)(2,1)S(1)}, u32[]{:S(2)}, u32[]{:S(2)}) collective-permute-start(bf16[64,2048]{1,0:T(8,128)(2,1)S(1)} %bitcast_convert_fusion), channel_id=1, source_target_pairs={{8,0},{16,8},{24,16},{32,24},{40,32},{48,40},{56,48},{64,56},{72,6... | collective-permute-start | bytes 786440 | tf_op jit(solution)/shard_map/ppermute | solution.py:22
  21.2 11.5 %collective-permute-start.3 = (bf16[64,2048]{1,0:T(8,128)(2,1)S(1)}, bf16[64,2048]{1,0:T(8,128)(2,1)S(1)}, u32[]{:S(2)}, u32[]{:S(2)}) collective-permute-start(bf16[64,2048]{1,0:T(8,128)(2,1)S(1)} %bitcast_convert_fusion), channel_id=1, source_target_pairs={{16,0},{24,8},{32,16},{40,24},{48,32},{56,40},{64,48},{72,56},{80,... | collective-permute-start | bytes 786440 | tf_op jit(solution)/shard_map/ppermute | solution.py:22
  50.9 14.3 %copy-start.1 = (f32[1,64,2048]{2,1,0:T(8,128)S(1)}, f32[1,64,2048]{2,1,0:T(8,128)}, u32[]{:S(2)}) copy-start(f32[1,64,2048]{2,1,0:T(8,128)} %param.7) | copy-start | bytes 1572868
  50.9 14.3 %copy-start.3 = (f32[1,64,2048]{2,1,0:T(8,128)S(1)}, f32[1,64,2048]{2,1,0:T(8,128)}, u32[]{:S(2)}) copy-start(f32[1,64,2048]{2,1,0:T(8,128)} %param.8) | copy-start | bytes 1572868
  63.3 12.6 %copy-start.4 = (s32[1,2048]{1,0:T(1,128)S(1)}, s32[1,2048]{1,0:T(1,128)}, u32[]{:S(2)}) copy-start(s32[1,2048]{1,0:T(1,128)} %param.11) | copy-start | bytes 24580
  66.0 9.8 %all-to-all-start = ((f32[2,1,2048]{2,1,0:T(1,128)}), f32[2,1,2048]{2,1,0:T(1,128)S(1)}, u32[]{:S(2)}, u32[]{:S(2)}) async-start(f32[2,1,2048]{2,1,0:T(1,128)} %broadcast_in_dim.67), calls=%async_computation | async-start | bytes 32768 | tf_op jit(solution)/shard_map/all_to_all | solution.py:27
  130.8 6.2 %copy-start.2 = (f32[1,64,2048]{2,1,0:T(8,128)}, f32[1,64,2048]{2,1,0:T(8,128)S(1)}, u32[]{:S(2)}) copy-start(f32[1,64,2048]{2,1,0:T(8,128)S(1)} %fusion.20) | copy-start | bytes 1572868
Sparse Core Ops, SparseCore 0:
  23.3 35.7 all-gather.2
where the time goes:
time: 169 us; the launch traced here: 168 us
  blocking collectives  62 us (37%)
  local copies, waits for them, and re-layouts  27.9 us (17%)
  matrix products  27 us (16%)
  starting transfers between devices  19.3 us (11%)
  between operations  14.3 us (8%)
  other arithmetic  11.1 us (7%)
  waiting for transfers between devices  6.85 us (4%)
    all_gather x1, blocking collectives, rows_first(): result, at, done = (lax.all_gather(both, axis, axis=0, tiled=True), 0, [])  42.7 us
    all_to_all x1, blocking collectives, sent_and_summed(): lax.all_to_all(parts, axis, split_axis=0, concat_axis=0, tiled=True)  19.3 us
    gather x24, local copies, waits for them, and re-layouts  18.1 us
    ppermute x4, starting transfers between devices, passed_along(): return lax.ppermute(block, axis, route)  14.8 us
    dot_general x1, matrix products, per_device(): jnp.einsum('ntw,nrw->tnr', windows, band_tiles, preferred_element_type=jn...  12.4 us
    dot_general x1, matrix products, per_device(): jnp.dot(same_group, trait_total, precision=lax.Precision.HIGHEST)  6.93 us
    dot_general x1, matrix products, per_device(): lax.dot_general(updated.astype(jnp.bfloat16), genotype, (((1,), (1,)), ((...  6.23 us
    all_to_all x1, waiting for transfers between devices, sent_to_all(): return lax.all_to_all(copies, axis, split_axis=0, concat_axis=0, tiled=True)  4.96 us
  transfers between devices with their start and end apart: 6, of which 2 were waited for; matrix products, arithmetic and copies ran while one was open for 23% of the time, Pallas kernels for 0%

commit v1 on v0

--- a/solution.py
+++ b/solution.py
@@ -9,6 +9,13 @@
 step_size = 0.5
 merging = 0.5
 epsilon = 1e-06
+
+
+def name_targets_now(buf, mesh_name, where_dim):
+    return jnp.concatenate(
+        lax.all_to_all(jnp.stack([buf for _ in range(lax.axis_size(mesh_name))]), mesh_name, 0, 0),
+        axis=where_dim,
+    )
 
 
 def total_of_pieces(value, axis):
@@ -34,7 +41,7 @@
 def rows_first(arrays, axis, dims):
     turned = [jnp.moveaxis(a, dim, 0) for a, dim in zip(arrays, dims)]
     both = jnp.concatenate([t.reshape(len(t), -1) for t in turned], axis=1)
-    result, at, done = (lax.all_gather(both, axis, axis=0, tiled=True), 0, [])
+    result, at, done = (name_targets_now(both, axis, 0), 0, [])
     for t, dim in zip(turned, dims):
         piece = result[:, at : at + t[0].size].reshape(-1, *t.shape[1:])
         done.append(jnp.moveaxis(piece, 0, dim))

time: 169 us -> 147 us (0.87)
  blocking collectives: 62 us -> 17.5 us
  starting transfers between devices: 19.3 us -> 31.8 us
  waiting for transfers between devices: 6.85 us -> 15.4 us
    all_gather x1 -> x0, blocking collectives: 42.7 us -> none  [rows_first(): result, at, done = (lax.all_gather(both, axis, axis=0, tiled=True), 0, [])]
    all_to_all x0 -> x1, starting transfers between devices: none -> 12.5 us  [name_targets_now(): lax.all_to_all(jnp.stack([buf for _ in range(lax.axis_size(mesh_name))]),...]
    all_to_all x0 -> x1, waiting for transfers between devices: none -> 8.06 us  [name_targets_now(): lax.all_to_all(jnp.stack([buf for _ in range(lax.axis_size(mesh_name))]),...]
    all_to_all x1, blocking collectives: 19.3 us -> 17.5 us  [sent_and_summed(): lax.all_to_all(parts, axis, split_axis=0, concat_axis=0, tiled=True)]
  transfers between devices with their start and end apart: 6 -> 7, of which waited for: 2 -> 3; matrix products, arithmetic and copies ran while one was open for 23% -> 27% of each run, Pallas kernels for 0% -> 0%
where the time goes in v1:
time: 147 us; the launch traced here: 145 us
  starting transfers between devices  31.8 us (22%)
  local copies, waits for them, and re-layouts  28.4 us (19%)
  matrix products  27 us (18%)
  blocking collectives  17.5 us (12%)
  waiting for transfers between devices  15.4 us (10%)
  between operations  14.3 us (10%)
  other arithmetic  11.1 us (8%)
    gather x24, local copies, waits for them, and re-layouts  18.1 us
    all_to_all x1, blocking collectives, sent_and_summed(): lax.all_to_all(parts, axis, split_axis=0, concat_axis=0, tiled=True)  17.5 us
    ppermute x4, starting transfers between devices, passed_along(): return lax.ppermute(block, axis, route)  14.8 us
    all_to_all x1, starting transfers between devices, name_targets_now(): lax.all_to_all(jnp.stack([buf for _ in range(lax.axis_size(mesh_name))]),...  12.5 us
    dot_general x1, matrix products, per_device(): jnp.einsum('ntw,nrw->tnr', windows, band_tiles, preferred_element_type=jn...  12.4 us
    all_to_all x1, waiting for transfers between devices, name_targets_now(): lax.all_to_all(jnp.stack([buf for _ in range(lax.axis_size(mesh_name))]),...  8.06 us
    dot_general x1, matrix products, per_device(): jnp.dot(same_group, trait_total, precision=lax.Precision.HIGHEST)  6.93 us
    dot_general x1, matrix products, per_device(): lax.dot_general(updated.astype(jnp.bfloat16), genotype, (((1,), (1,)), ((...  6.23 us
  transfers between devices with their start and end apart: 7, of which 3 were waited for; matrix products, arithmetic and copies ran while one was open for 27% of the time, Pallas kernels for 0%

profile of v1, /device:TPU:32, one launch (start us, length us, event | category | flops | bytes accessed | tf_op | source)
XLA Modules:
  0.0 145.5 jit_solution(9786577859912836264)
XLA Ops:
  8.3 4.9 %collective-permute-start = (bf16[64,2048]{1,0:T(8,128)(2,1)S(1)}, bf16[64,2048]{1,0:T(8,128)(2,1)S(1)}, u32[]{:S(2)}, u32[]{:S(2)}) collective-permute-start(bf16[64,2048]{1,0:T(8,128)(2,1)S(1)} %bitcast_convert_fusion), channel_id=1, source_target_pairs={{0,16},{8,24},{16,32},{24,40},{32,48},{40,56},{48,64},{56,72},{64,... | collective-permute-start | bytes 786440 | tf_op jit(solution)/shard_map/ppermute | solution.py:29
  13.2 2.5 %collective-permute-start.1 = (bf16[64,2048]{1,0:T(8,128)(2,1)S(1)}, bf16[64,2048]{1,0:T(8,128)(2,1)S(1)}, u32[]{:S(2)}, u32[]{:S(2)}) collective-permute-start(bf16[64,2048]{1,0:T(8,128)(2,1)S(1)} %bitcast_convert_fusion), channel_id=1, source_target_pairs={{0,8},{8,16},{16,24},{24,32},{32,40},{40,48},{48,56},{56,64},{64,7... | collective-permute-start | bytes 786440 | tf_op jit(solution)/shard_map/ppermute | solution.py:29
  15.7 5.5 %collective-permute-start.2 = (bf16[64,2048]{1,0:T(8,128)(2,1)S(1)}, bf16[64,2048]{1,0:T(8,128)(2,1)S(1)}, u32[]{:S(2)}, u32[]{:S(2)}) collective-permute-start(bf16[64,2048]{1,0:T(8,128)(2,1)S(1)} %bitcast_convert_fusion), channel_id=1, source_target_pairs={{8,0},{16,8},{24,16},{32,24},{40,32},{48,40},{56,48},{64,56},{72,6... | collective-permute-start | bytes 786440 | tf_op jit(solution)/shard_map/ppermute | solution.py:29
  21.2 1.9 %collective-permute-start.3 = (bf16[64,2048]{1,0:T(8,128)(2,1)S(1)}, bf16[64,2048]{1,0:T(8,128)(2,1)S(1)}, u32[]{:S(2)}, u32[]{:S(2)}) collective-permute-start(bf16[64,2048]{1,0:T(8,128)(2,1)S(1)} %bitcast_convert_fusion), channel_id=1, source_target_pairs={{16,0},{24,8},{32,16},{40,24},{48,32},{56,40},{64,48},{72,56},{80,... | collective-permute-start | bytes 786440 | tf_op jit(solution)/shard_map/ppermute | solution.py:29
  23.9 2.5 %fusion.2 = f32[2048]{0:T(1024)S(1)} fusion(s32[2048]{0:T(1024)} %bitcast.94), kind=kLoop, calls=%fused_computation.5 | loop fusion | flops 12580864 | bytes 16384 | tf_op jit(solution)/shard_map/reduce_sum | solution.py:100
  30.3 2.5 %collective-permute-done.3 = bf16[64,2048]{1,0:T(8,128)(2,1)S(1)} collective-permute-done((bf16[64,2048]{1,0:T(8,128)(2,1)S(1)}, bf16[64,2048]{1,0:T(8,128)(2,1)S(1)}, u32[]{:S(2)}, u32[]{:S(2)}) %collective-permute-start.3) | collective-permute-done | bytes 262176 | tf_op jit(solution)/shard_map/ppermute | solution.py:29
  32.8 18.2 %while.1 = (s32[]{:T(128)}, bf16[64,10240]{1,0:T(8,128)(2,1)S(1)}, s32[8,2]{0,1:T(2,128)S(1)}, bf16[8,64,4096]{2,1,0:T(8,128)(2,1)}, s32[]{:T(128)}) while((s32[]{:T(128)}, bf16[64,10240]{1,0:T(8,128)(2,1)S(1)}, s32[8,2]{0,1:T(2,128)S(1)}, bf16[8,64,4096]{2,1,0:T(8,128)(2,1)}, s32[]{:T(128)}) %tuple.29), condition=%wide.while_cond, body=%wide.while_body.sunk | while | flops 2 | bytes 1049689 | solution.py:89
  35.7 1.7 %bitcast_dynamic-update-slice_fusion.2 = bf16[8,64,4096]{2,1,0:T(8,128)(2,1)} fusion(bf16[8,64,4096]{2,1,0:T(8,128)(2,1)} %get-tuple-element.65, s32[]{:T(128)} %get-tuple-element.62, bf16[64,10240]{1,0:T(8,128)(2,1)S(1)} %get-tuple-element.68, s32[]{:T(128)} %bitcast.82), kind=kLoop, calls=%fused_computation.clone.1 | loop fusion | bytes 1049600 | tf_op jit(solution)/shard_map/vmap()/gather
  37.9 1.7 %bitcast_dynamic-update-slice_fusion.2 = bf16[8,64,4096]{2,1,0:T(8,128)(2,1)} fusion(bf16[8,64,4096]{2,1,0:T(8,128)(2,1)} %get-tuple-element.65, s32[]{:T(128)} %get-tuple-element.62, bf16[64,10240]{1,0:T(8,128)(2,1)S(1)} %get-tuple-element.68, s32[]{:T(128)} %bitcast.82), kind=kLoop, calls=%fused_computation.clone.1 | loop fusion | bytes 1049600 | tf_op jit(solution)/shard_map/vmap()/gather
  40.2 1.7 %bitcast_dynamic-update-slice_fusion.2 = bf16[8,64,4096]{2,1,0:T(8,128)(2,1)} fusion(bf16[8,64,4096]{2,1,0:T(8,128)(2,1)} %get-tuple-element.65, s32[]{:T(128)} %get-tuple-element.62, bf16[64,10240]{1,0:T(8,128)(2,1)S(1)} %get-tuple-element.68, s32[]{:T(128)} %bitcast.82), kind=kLoop, calls=%fused_computation.clone.1 | loop fusion | bytes 1049600 | tf_op jit(solution)/shard_map/vmap()/gather
  42.5 1.6 %bitcast_dynamic-update-slice_fusion.2 = bf16[8,64,4096]{2,1,0:T(8,128)(2,1)} fusion(bf16[8,64,4096]{2,1,0:T(8,128)(2,1)} %get-tuple-element.65, s32[]{:T(128)} %get-tuple-element.62, bf16[64,10240]{1,0:T(8,128)(2,1)S(1)} %get-tuple-element.68, s32[]{:T(128)} %bitcast.82), kind=kLoop, calls=%fused_computation.clone.1 | loop fusion | bytes 1049600 | tf_op jit(solution)/shard_map/vmap()/gather
  44.7 1.7 %bitcast_dynamic-update-slice_fusion.2 = bf16[8,64,4096]{2,1,0:T(8,128)(2,1)} fusion(bf16[8,64,4096]{2,1,0:T(8,128)(2,1)} %get-tuple-element.65, s32[]{:T(128)} %get-tuple-element.62, bf16[64,10240]{1,0:T(8,128)(2,1)S(1)} %get-tuple-element.68, s32[]{:T(128)} %bitcast.82), kind=kLoop, calls=%fused_computation.clone.1 | loop fusion | bytes 1049600 | tf_op jit(solution)/shard_map/vmap()/gather
  49.3 1.7 %bitcast_dynamic-update-slice_fusion.2 = bf16[8,64,4096]{2,1,0:T(8,128)(2,1)} fusion(bf16[8,64,4096]{2,1,0:T(8,128)(2,1)} %get-tuple-element.65, s32[]{:T(128)} %get-tuple-element.62, bf16[64,10240]{1,0:T(8,128)(2,1)S(1)} %get-tuple-element.68, s32[]{:T(128)} %bitcast.82), kind=kLoop, calls=%fused_computation.clone.1 | loop fusion | bytes 1049600 | tf_op jit(solution)/shard_map/vmap()/gather
  50.9 12.4 %fusion.33 = f32[8,64,256]{2,1,0:T(8,128)S(1)} fusion(bf16[8,64,4096]{2,1,0:T(8,128)(2,1)} %get-tuple-element.9, bf16[8,256,4096]{2,1,0:T(8,128)(2,1)} %bitcast.83), kind=kOutput, calls=%fused_computation.59 | convolution fusion | flops 1073741824 | bytes 21495808 | tf_op jit(solution)/shard_map/ntw,nrw->tnr/dot_general | solution.py:92
  63.4 1.8 %reduce_sum.63 = f32[64,2048]{1,0:T(8,128)S(1)} reduce(f32[4,64,2048]{2,1,0:T(8,128)} %all-gather.2.cloned.1.call-done, f32[]{:T(128)} %constant.8.clone.1), dimensions={0}, to_apply=%region_0.0 | reduce | flops 393216 | bytes 2621444 | tf_op jit(solution)/shard_map/reduce_sum | solution.py:23
  66.0 4.4 %all-to-all-start = ((f32[2,1,2048]{2,1,0:T(1,128)}), f32[2,1,2048]{2,1,0:T(1,128)S(1)}, u32[]{:S(2)}, u32[]{:S(2)}) async-start(f32[2,1,2048]{2,1,0:T(1,128)} %broadcast_in_dim.67), calls=%async_computation | async-start | bytes 32768 | tf_op jit(solution)/shard_map/all_to_all | solution.py:34
  71.1 4.8 %all-to-all-done = f32[2,1,2048]{2,1,0:T(1,128)S(1)} async-done(((f32[2,1,2048]{2,1,0:T(1,128)}), f32[2,1,2048]{2,1,0:T(1,128)S(1)}, u32[]{:S(2)}, u32[]{:S(2)}) %all-to-all-start) | async-done | bytes 16416 | tf_op jit(solution)/shard_map/all_to_all | solution.py:34
  75.9 6.9 %fusion = f32[1,2048]{1,0:T(1,128)S(1)} fusion(f32[2048,1]{0,1:T(1,128)S(1)} %bitcast.92, s32[2048]{0:T(1024)S(1)} %bitcast.96), kind=kOutput, calls=%fused_computation.2 | convolution fusion | flops 54525952 | bytes 24576 | tf_op jit(solution)/shard_map/dot_general | solution.py:99
  83.4 3.8 %concatenate.13 = f32[1,6]{1,0:T(1,128)S(1)} concatenate(f32[1,1]{1,0:T(1,128)} %bitcast.10, f32[1,1]{1,0:T(1,128)} %bitcast.11, f32[1,1]{1,0:T(1,128)} %bitcast.15, f32[1,1]{1,0:T(1,128)} %bitcast.16, f32[1,1]{1,0:T(1,128)} %bitcast.17, f32[1,1]{1,0:T(1,128)} %bitcast.18), dimensions={1} | concatenate | bytes 48 | tf_op jit(solution)/shard_map/concatenate | solution.py:43
  87.9 12.5 %all-to-all-start.1 = ((f32[32,1,6]{2,1,0:T(1,128)}), f32[32,1,6]{2,1,0:T(1,128)S(1)}, u32[]{:S(2)}, u32[]{:S(2)}) async-start(f32[32,1,6]{2,1,0:T(1,128)} %stack.2), calls=%async_computation.1 | async-start | bytes 32768 | tf_op jit(solution)/shard_map/all_to_all | solution.py:16
  100.9 8.1 %all-to-all-done.1 = f32[32,1,6]{2,1,0:T(1,128)S(1)} async-done(((f32[32,1,6]{2,1,0:T(1,128)}), f32[32,1,6]{2,1,0:T(1,128)S(1)}, u32[]{:S(2)}, u32[]{:S(2)}) %all-to-all-start.1) | async-done | bytes 800 | tf_op jit(solution)/shard_map/all_to_all | solution.py:16
  109.6 6.2 %fusion.7 = f32[64,2048]{1,0:T(8,128)S(1)} fusion(bf16[1,2048,2048]{2,1,0:T(8,128)(2,1)} %param.13, f32[1,64,2048]{2,1,0:T(8,128)S(1)} %fusion.20), kind=kOutput, calls=%fused_computation.10 | convolution fusion | flops 537133056 | bytes 9437184 | tf_op jit(solution)/shard_map/dot_general | solution.py:138
  117.5 17.5 %all_to_all.16 = f32[32,1,4096]{2,1,0:T(1,128)S(1)} all-to-all(f32[32,1,4096]{2,1,0:T(1,128)S(1)} %reshape.140), channel_id=1, replica_groups=mesh['genome'=32,'anc'=4,'trait'=2] {'genome'}, dimensions={0} | all-to-all | bytes 1048576 | tf_op jit(solution)/shard_map/all_to_all | solution.py:60
  135.6 1.9 %reduce.13 = f32[32,4096]{1,0:T(8,128)S(1)} reduce(f32[32,1,4096]{2,1,0:T(1,128)S(1)} %all_to_all.16, f32[]{:T(128)} %broadcast.113), dimensions={1}, to_apply=%all_to_all.12.reduce_sub_computation | reduce | bytes 1048580 | tf_op jit(solution)/shard_map/all_to_all | solution.py:60
  (66 shorter events, 20.9 us)
Async XLA Ops:
  7.2 19.3 %copy-start = (f32[1,64]{1,0:T(1,128)S(1)}, f32[1,64]{1,0:T(1,128)}, u32[]{:S(2)}) copy-start(f32[1,64]{1,0:T(1,128)} %param.12) | copy-start | bytes 772
  7.2 56.2 %all-gather.2.cloned.1.call-start = ((), (), s32[]{:S(2)}) async-start(), calls=%async_computation.3 | async-start | bytes 2621440 | tf_op jit(solution)/shard_map/all_gather | solution.py:22
  8.3 20.8 %collective-permute-start = (bf16[64,2048]{1,0:T(8,128)(2,1)S(1)}, bf16[64,2048]{1,0:T(8,128)(2,1)S(1)}, u32[]{:S(2)}, u32[]{:S(2)}) collective-permute-start(bf16[64,2048]{1,0:T(8,128)(2,1)S(1)} %bitcast_convert_fusion), channel_id=1, source_target_pairs={{0,16},{8,24},{16,32},{24,40},{32,48},{40,56},{48,64},{56,72},{64,... | collective-permute-start | bytes 786440 | tf_op jit(solution)/shard_map/ppermute | solution.py:29
  13.2 15.9 %collective-permute-start.1 = (bf16[64,2048]{1,0:T(8,128)(2,1)S(1)}, bf16[64,2048]{1,0:T(8,128)(2,1)S(1)}, u32[]{:S(2)}, u32[]{:S(2)}) collective-permute-start(bf16[64,2048]{1,0:T(8,128)(2,1)S(1)} %bitcast_convert_fusion), channel_id=1, source_target_pairs={{0,8},{8,16},{16,24},{24,32},{32,40},{40,48},{48,56},{56,64},{64,7... | collective-permute-start | bytes 786440 | tf_op jit(solution)/shard_map/ppermute | solution.py:29
  15.7 14.5 %collective-permute-start.2 = (bf16[64,2048]{1,0:T(8,128)(2,1)S(1)}, bf16[64,2048]{1,0:T(8,128)(2,1)S(1)}, u32[]{:S(2)}, u32[]{:S(2)}) collective-permute-start(bf16[64,2048]{1,0:T(8,128)(2,1)S(1)} %bitcast_convert_fusion), channel_id=1, source_target_pairs={{8,0},{16,8},{24,16},{32,24},{40,32},{48,40},{56,48},{64,56},{72,6... | collective-permute-start | bytes 786440 | tf_op jit(solution)/shard_map/ppermute | solution.py:29
  21.2 11.5 %collective-permute-start.3 = (bf16[64,2048]{1,0:T(8,128)(2,1)S(1)}, bf16[64,2048]{1,0:T(8,128)(2,1)S(1)}, u32[]{:S(2)}, u32[]{:S(2)}) collective-permute-start(bf16[64,2048]{1,0:T(8,128)(2,1)S(1)} %bitcast_convert_fusion), channel_id=1, source_target_pairs={{16,0},{24,8},{32,16},{40,24},{48,32},{56,40},{64,48},{72,56},{80,... | collective-permute-start | bytes 786440 | tf_op jit(solution)/shard_map/ppermute | solution.py:29
  50.9 14.3 %copy-start.1 = (f32[1,64,2048]{2,1,0:T(8,128)S(1)}, f32[1,64,2048]{2,1,0:T(8,128)}, u32[]{:S(2)}) copy-start(f32[1,64,2048]{2,1,0:T(8,128)} %param.7) | copy-start | bytes 1572868
  50.9 14.3 %copy-start.3 = (f32[1,64,2048]{2,1,0:T(8,128)S(1)}, f32[1,64,2048]{2,1,0:T(8,128)}, u32[]{:S(2)}) copy-start(f32[1,64,2048]{2,1,0:T(8,128)} %param.8) | copy-start | bytes 1572868
  63.3 12.6 %copy-start.4 = (s32[1,2048]{1,0:T(1,128)S(1)}, s32[1,2048]{1,0:T(1,128)}, u32[]{:S(2)}) copy-start(s32[1,2048]{1,0:T(1,128)} %param.11) | copy-start | bytes 24580
  66.0 9.8 %all-to-all-start = ((f32[2,1,2048]{2,1,0:T(1,128)}), f32[2,1,2048]{2,1,0:T(1,128)S(1)}, u32[]{:S(2)}, u32[]{:S(2)}) async-start(f32[2,1,2048]{2,1,0:T(1,128)} %broadcast_in_dim.67), calls=%async_computation | async-start | bytes 32768 | tf_op jit(solution)/shard_map/all_to_all | solution.py:34
  87.9 21.0 %all-to-all-start.1 = ((f32[32,1,6]{2,1,0:T(1,128)}), f32[32,1,6]{2,1,0:T(1,128)S(1)}, u32[]{:S(2)}, u32[]{:S(2)}) async-start(f32[32,1,6]{2,1,0:T(1,128)} %stack.2), calls=%async_computation.1 | async-start | bytes 32768 | tf_op jit(solution)/shard_map/all_to_all | solution.py:16
  109.6 6.2 %copy-start.2 = (f32[1,64,2048]{2,1,0:T(8,128)}, f32[1,64,2048]{2,1,0:T(8,128)S(1)}, u32[]{:S(2)}) copy-start(f32[1,64,2048]{2,1,0:T(8,128)S(1)} %fusion.20) | copy-start | bytes 1572868
Sparse Core Ops, SparseCore 0:
  23.3 35.7 all-gather.1
